TPU v7x, 32 devices: a whole 2x2x4 slice. The times are simulated.
32 devices in a mesh: wide: 8 (over y, x, core), narrow: 4 (over z).
Axes of the slice: x: 2, y: 2, z: 4, core: 2. Of those that a mesh axis runs over, the one named last changes fastest.
Arguments:
- amplitudes: float32 [2, 8, 8, 4, 128, 128], P(None, None, 'wide', 'narrow'), may hold values from -6 to 6
- gates: float32 [3, 2, 2, 128, 128], replicated, may hold values from -0.375 to 0.375
Outputs:
- final_state: float32 [2, 8, 8, 4, 128, 128], P(None, None, 'wide', 'narrow')
All inputs are finite; a program needn't handle non-finite values.
Results may differ from a plain program's by a relative error of at most 0.0001.
Values sent between devices are 32-bit elements; how exact they have to be, the bound alone decides.
A program may use at most 64 MiB of HBM per device.

v0:
```python
import jax
import jax.numpy as jnp
from jax import lax
from jax.sharding import PartitionSpec as P

precise = lax.Precision.HIGHEST


def blocks(matrix):
    return jnp.stack([jnp.stack([matrix[0], -matrix[1]]), jnp.stack([matrix[1], matrix[0]])])


def on_rows(vector, matrix):
    return jnp.einsum("cdjk,drkb->crjb", blocks(matrix), vector, precision=precise)


def on_columns(vector, matrix):
    return jnp.einsum("cdjk,drak->craj", blocks(matrix), vector, precision=precise)


def shards(amplitudes, gates):
    layout = amplitudes.shape
    slab_count = layout[1]
    gate_order = layout[4]
    vector = amplitudes.reshape(2, slab_count, gate_order, gate_order)
    vector = on_rows(vector, gates[0, 0])
    vector = on_columns(vector, gates[0, 1])
    resident = vector.reshape(layout)
    arrived = lax.all_to_all(resident, "wide", split_axis=4, concat_axis=2, tiled=True)
    items_here = arrived.shape[1]
    slab_data = arrived.reshape(2, items_here, gate_order, gate_order)
    slab_data = on_rows(slab_data, gates[1, 0])
    slab_data = on_columns(slab_data, gates[1, 1])
    resident = slab_data.reshape(2, items_here, 1, 1, gate_order, gate_order)
    arrived = lax.all_to_all(resident, "narrow", split_axis=4, concat_axis=3, tiled=True)
    vector = arrived.reshape(2, slab_count, gate_order, gate_order)
    vector = on_rows(vector, gates[2, 0])
    vector = on_columns(vector, gates[2, 1])
    return vector.reshape(layout)


def solution(mesh):
    return jax.shard_map(
        shards,
        mesh=mesh,
        in_specs=(P(None, None, "wide", "narrow", None, None), P()),
        out_specs=P(None, None, "wide", "narrow", None, None),
        check_vma=False,
    )
```

profile of v0, /device:TPU:0, one launch (start us, length us, event | category | flops | bytes accessed | tf_op | source)
XLA Modules:
  0.0 61.8 jit_solution(2130488809126210702)
XLA Ops:
  0.0 0.0 copy-start
  0.0 0.0 copy-start.1
  0.0 1.3 %slice_bitcast_fusion = (f32[1,128,128]{2,1,0:T(8,128)S(1)}, f32[1,128,128]{2,1,0:T(8,128)S(1)}, f32[1,128,128]{2,1,0:T(8,128)S(1)}, f32[1,128,128]{2,1,0:T(8,12...) fusion(f32[3,2,2,128,128]{4,3,2,1,0:T(8,128)} %param.3), kind=kLoop, calls=%fused_computation.39 | loop fusion | bytes 1572864 | tf_op jit(solution)/shard_map/squeeze | solution.py:10
  1.3 0.2 copy-done.1
  1.6 0.2 copy-done
  1.8 1.0 %convolution_bitcast_fusion.5 = f32[2,8,128,128,1]{3,2,0,4,1:T(8,128)S(1)} fusion(f32[1,2,128,128]{3,2,1,0:T(8,128)S(1)} %get-tuple-element.34, f32[1,2,128,128]{3,2,1,0:T(8,128)S(1)} %get-tuple-element.33, f32[2,8,1,1,128,128]{5,4,3,2,1,0:T(8,128)S(1)} %copy-done), kind=kOutput, calls=%fused_computation.5 | convolution fusion | flops 805371904 | bytes 2359296 | tf_op jit(solution)/shard_map/cdjk,drkb->crjb/dot_general | solution.py:14
  2.8 1.0 %convolution_bitcast_fusion.4 = f32[2,8,1,1,128,128]{5,4,0,1,3,2:T(8,128)S(1)} fusion(f32[2,8,128,128,1]{3,2,0,4,1:T(8,128)S(1)} %convolution_bitcast_fusion.5, f32[1,2,128,128]{3,2,1,0:T(8,128)S(1)} %get-tuple-element.35, f32[1,2,128,128]{3,2,1,0:T(8,128)S(1)} %get-tuple-element.36), kind=kOutput, calls=%fused_computation.4 | convolution fusion | flops 805371904 | bytes 2359296 | tf_op jit(solution)/shard_map/cdjk,drak->craj/dot_general | solution.py:18
  3.9 1.8 %copy.4 = f32[2,8,1,1,128,128]{5,0,1,3,2,4:T(2,128)} copy(f32[2,8,1,1,128,128]{5,4,0,1,3,2:T(8,128)S(1)} %convolution_bitcast_fusion.4) | data formatting | bytes 2097152 | tf_op jit(solution)/shard_map/reshape | solution.py:28
  5.6 5.2 %all-to-all-start = ((f32[2,8,1,1,128,128]{5,0,1,3,2,4:T(2,128)}), f32[2,8,1,1,128,128]{5,0,1,3,2,4:T(2,128)S(1)}, u32[]{:S(2)}, u32[]{:S(2)}) async-start(f32[2,8,1,1,128,128]{5,0,1,3,2,4:T(2,128)} %copy.4), calls=%async_computation | async-start | bytes 2097152 | tf_op jit(solution)/shard_map/all_to_all | solution.py:29
  10.9 15.3 %all-to-all-done = f32[2,8,1,1,128,128]{5,0,1,3,2,4:T(2,128)S(1)} async-done(((f32[2,8,1,1,128,128]{5,0,1,3,2,4:T(2,128)}), f32[2,8,1,1,128,128]{5,0,1,3,2,4:T(2,128)S(1)}, u32[]{:S(2)}, u32[]{:S(2)}) %all-to-all-start) | async-done | bytes 1048608 | tf_op jit(solution)/shard_map/all_to_all | solution.py:29
  26.2 1.4 %convolution_bitcast_fusion.3 = f32[2,8,128,128,1]{3,2,0,4,1:T(8,128)S(1)} fusion(f32[2,8,128,128,1]{3,0,1,2,4:T(2,128)S(1)} %bitcast.142, f32[1,2,128,128]{3,2,1,0:T(8,128)S(1)} %get-tuple-element.30, f32[1,2,128,128]{3,2,1,0:T(8,128)S(1)} %get-tuple-element.29), kind=kOutput, calls=%fused_computation.3 | convolution fusion | flops 805371904 | bytes 2359296 | tf_op jit(solution)/shard_map/cdjk,drkb->crjb/dot_general | solution.py:14
  27.6 1.0 %convolution_bitcast_fusion.2 = f32[2,8,1,1,128,128]{5,4,0,1,3,2:T(8,128)S(1)} fusion(f32[2,8,128,128,1]{3,2,0,4,1:T(8,128)S(1)} %convolution_bitcast_fusion.3, f32[1,2,128,128]{3,2,1,0:T(8,128)S(1)} %get-tuple-element.37, f32[1,2,128,128]{3,2,1,0:T(8,128)S(1)} %get-tuple-element.38), kind=kOutput, calls=%fused_computation.2 | convolution fusion | flops 805371904 | bytes 2359296 | tf_op jit(solution)/shard_map/cdjk,drak->craj/dot_general | solution.py:18
  28.7 1.8 %copy.5 = f32[2,8,1,1,128,128]{5,0,1,3,2,4:T(2,128)} copy(f32[2,8,1,1,128,128]{5,4,0,1,3,2:T(8,128)S(1)} %convolution_bitcast_fusion.2) | data formatting | bytes 2097152 | tf_op jit(solution)/shard_map/reshape | solution.py:34
  30.4 4.9 %all-to-all-start.1 = ((f32[2,8,1,1,128,128]{5,0,1,3,2,4:T(2,128)}), f32[2,8,1,1,128,128]{5,0,1,3,2,4:T(2,128)S(1)}, u32[]{:S(2)}, u32[]{:S(2)}) async-start(f32[2,8,1,1,128,128]{5,0,1,3,2,4:T(2,128)} %copy.5), calls=%async_computation.1 | async-start | bytes 2097152 | tf_op jit(solution)/shard_map/all_to_all | solution.py:35
  35.4 22.9 %all-to-all-done.1 = f32[2,8,1,1,128,128]{5,0,1,3,2,4:T(2,128)S(1)} async-done(((f32[2,8,1,1,128,128]{5,0,1,3,2,4:T(2,128)}), f32[2,8,1,1,128,128]{5,0,1,3,2,4:T(2,128)S(1)}, u32[]{:S(2)}, u32[]{:S(2)}) %all-to-all-start.1) | async-done | bytes 1048608 | tf_op jit(solution)/shard_map/all_to_all | solution.py:35
  58.3 1.4 %convolution_bitcast_fusion.1 = f32[2,8,128,128,1]{3,2,0,4,1:T(8,128)S(1)} fusion(f32[2,8,128,128,1]{3,0,1,2,4:T(2,128)S(1)} %bitcast.141, f32[1,2,128,128]{3,2,1,0:T(8,128)S(1)} %get-tuple-element.26, f32[1,2,128,128]{3,2,1,0:T(8,128)S(1)} %get-tuple-element.25), kind=kOutput, calls=%fused_computation.1 | convolution fusion | flops 805371904 | bytes 2359296 | tf_op jit(solution)/shard_map/cdjk,drkb->crjb/dot_general | solution.py:14
  59.7 1.0 %convolution_bitcast_fusion = f32[2,8,1,1,128,128]{5,4,0,1,3,2:T(8,128)S(1)} fusion(f32[2,8,128,128,1]{3,2,0,4,1:T(8,128)S(1)} %convolution_bitcast_fusion.1, f32[1,2,128,128]{3,2,1,0:T(8,128)S(1)} %get-tuple-element.39, f32[1,2,128,128]{3,2,1,0:T(8,128)S(1)} %get-tuple-element.40), kind=kOutput, calls=%fused_computation | convolution fusion | flops 805371904 | bytes 2359296 | tf_op jit(solution)/shard_map/cdjk,drak->craj/dot_general | solution.py:18
  60.7 1.1 %copy.6 = f32[2,8,1,1,128,128]{5,4,3,2,1,0:T(8,128)} copy(f32[2,8,1,1,128,128]{5,4,0,1,3,2:T(8,128)S(1)} %convolution_bitcast_fusion) | data formatting | bytes 2097152 | tf_op jit(solution)/shard_map/reshape | solution.py:39
  (4 shorter events, 0.1 us)
Async XLA Ops:
  0.0 1.8 %copy-start = (f32[2,8,1,1,128,128]{5,4,3,2,1,0:T(8,128)S(1)}, f32[2,8,1,1,128,128]{5,4,3,2,1,0:T(8,128)}, u32[]{:S(2)}) copy-start(f32[2,8,1,1,128,128]{5,4,3,2,1,0:T(8,128)} %param.2) | copy-start | bytes 3145732
  0.0 1.5 %copy-start.1 = (f32[3,2,2,128,128]{4,3,2,1,0:T(8,128)S(1)}, f32[3,2,2,128,128]{4,3,2,1,0:T(8,128)}, u32[]{:S(2)}) copy-start(f32[3,2,2,128,128]{4,3,2,1,0:T(8,128)} %param.3) | copy-start | bytes 2359300
  5.6 20.6 %all-to-all-start = ((f32[2,8,1,1,128,128]{5,0,1,3,2,4:T(2,128)}), f32[2,8,1,1,128,128]{5,0,1,3,2,4:T(2,128)S(1)}, u32[]{:S(2)}, u32[]{:S(2)}) async-start(f32[2,8,1,1,128,128]{5,0,1,3,2,4:T(2,128)} %copy.4), calls=%async_computation | async-start | bytes 2097152 | tf_op jit(solution)/shard_map/all_to_all | solution.py:29
  30.4 27.8 %all-to-all-start.1 = ((f32[2,8,1,1,128,128]{5,0,1,3,2,4:T(2,128)}), f32[2,8,1,1,128,128]{5,0,1,3,2,4:T(2,128)S(1)}, u32[]{:S(2)}, u32[]{:S(2)}) async-start(f32[2,8,1,1,128,128]{5,0,1,3,2,4:T(2,128)} %copy.5), calls=%async_computation.1 | async-start | bytes 2097152 | tf_op jit(solution)/shard_map/all_to_all | solution.py:35
where the time goes:
time: 62.6 us; the launch traced here: 61.8 us
  waiting for transfers between devices  38.3 us (61%)
  starting transfers between devices  10.1 us (16%)
  matrix products  6.91 us (11%)
  local copies, waits for them, and re-layouts  6.33 us (10%)
    all_to_all x1, waiting for transfers between devices, shards(): lax.all_to_all(resident, 'narrow', split_axis=4, concat_axis=3, tiled=True)  22.9 us
    all_to_all x1, waiting for transfers between devices, shards(): lax.all_to_all(resident, 'wide', split_axis=4, concat_axis=2, tiled=True)  15.3 us
    all_to_all x1, starting transfers between devices, shards(): lax.all_to_all(resident, 'wide', split_axis=4, concat_axis=2, tiled=True)  5.2 us
    all_to_all x1, starting transfers between devices, shards(): lax.all_to_all(resident, 'narrow', split_axis=4, concat_axis=3, tiled=True)  4.87 us
    dot_general x3, matrix products, on_rows(): jnp.einsum('cdjk,drkb->crjb', blocks(matrix), vector, precision=precise)  3.84 us
    dot_general x3, matrix products, on_columns(): jnp.einsum('cdjk,drak->craj', blocks(matrix), vector, precision=precise)  3.07 us
    reshape x1, local copies, waits for them, and re-layouts, shards(): resident = vector.reshape(layout)  1.78 us
    reshape x1, local copies, waits for them, and re-layouts, shards(): resident = slab_data.reshape(2, items_here, 1, 1, gate_order, gate_order)  1.78 us
  transfers between devices with their start and end apart: 2, of which 2 were waited for; matrix products, arithmetic and copies ran while one was open for 0% of the time, Pallas kernels for 0%

commit v1 on v0

v1 whole, which is shorter than its diff:
```python
import functools

import jax
import jax.numpy as jnp
from jax import lax
from jax.experimental import pallas as pl
from jax.experimental.pallas import tpu as pltpu
from jax.sharding import PartitionSpec as P

precise = lax.Precision.HIGHEST
MESH = pl.DeviceIdType.MESH
F32 = jnp.float32
BF16 = jnp.bfloat16


def blocks(matrix):
    return jnp.stack([jnp.stack([matrix[0], -matrix[1]]), jnp.stack([matrix[1], matrix[0]])])


def on_rows(vector, matrix):
    return jnp.einsum("cdjk,drkb->crjb", blocks(matrix), vector, precision=precise)


def on_columns(vector, matrix):
    return jnp.einsum("cdjk,drak->craj", blocks(matrix), vector, precision=precise)


def plain(amplitudes, gates):
    layout = amplitudes.shape
    slabs, order = layout[1], layout[4]
    vector = amplitudes.reshape(2, slabs, order, order)
    vector = on_columns(on_rows(vector, gates[0, 0]), gates[0, 1])
    vector = lax.all_to_all(vector.reshape(layout), "wide", split_axis=4, concat_axis=2, tiled=True)
    vector = vector.reshape(2, slabs, order, order)
    vector = on_columns(on_rows(vector, gates[1, 0]), gates[1, 1])
    vector = lax.all_to_all(vector.reshape(layout), "narrow", split_axis=4, concat_axis=3, tiled=True)
    vector = vector.reshape(2, slabs, order, order)
    vector = on_columns(on_rows(vector, gates[2, 0]), gates[2, 1])
    return vector.reshape(layout)


def partner(me, mask, count):
    out, bit = 0, 1
    while bit < count:
        digit = me // bit % 2
        if mask & bit:
            digit = 1 - digit
        out = out + digit * bit
        bit *= 2
    return out


def far_first(count):
    return sorted(range(1, count), key=lambda m: (-bin(m >> 1).count("1"), -m))


def split(value):
    high = value.astype(BF16)
    return high, (value - high.astype(F32)).astype(BF16)


def real_form(matrix):
    re, im = matrix[0], matrix[1]
    return jnp.concatenate(
        [jnp.concatenate([re, -im], axis=1), jnp.concatenate([im, re], axis=1)], axis=0
    )


def kernel(wide, narrow, amp, gates, out, x, g, y, yr, z, zr, left, right,
           load_sem, gate_sem, ws_sem, wr_sem, ns_sem, nr_sem):
    slabs, order = x.shape[1], x.shape[2]
    hw, hn = order // wide, order // narrow
    w, n = lax.axis_index("wide"), lax.axis_index("narrow")
    wide_masks = far_first(wide)
    narrow_masks = sorted(range(1, narrow), reverse=True)

    barrier = pltpu.get_barrier_semaphore()
    for mask in wide_masks:
        pl.semaphore_signal(barrier, inc=1, device_id=(partner(w, mask, wide), n), device_id_type=MESH)
    for mask in narrow_masks:
        pl.semaphore_signal(barrier, inc=1, device_id=(w, partner(n, mask, narrow)), device_id_type=MESH)

    def load(c):
        return pltpu.make_async_copy(amp.at[:, c], x.at[:, c], load_sem.at[c])

    def load_gate(t, k):
        return pltpu.make_async_copy(gates.at[t, k], g.at[t, k], gate_sem.at[t, k])

    load_gate(0, 0).start()
    load(0).start()
    for t in range(3):
        for k in range(2):
            if (t, k) != (0, 0):
                load_gate(t, k).start()
    for c in range(1, slabs):
        load(c).start()

    def send_wide(c, i):
        there = partner(w, wide_masks[i], wide)
        return pltpu.make_async_remote_copy(
            src_ref=y.at[c, :, pl.ds(pl.multiple_of(there * hw, hw), hw), :],
            dst_ref=yr.at[c, :, pl.ds(pl.multiple_of(w * hw, hw), hw), :],
            send_sem=ws_sem.at[c, i], recv_sem=wr_sem.at[c, i],
            device_id=(there, n), device_id_type=MESH)

    def send_narrow(c, i):
        there = partner(n, narrow_masks[i], narrow)
        return pltpu.make_async_remote_copy(
            src_ref=z.at[c, :, pl.ds(pl.multiple_of(there * hn, hn), hn), :],
            dst_ref=zr.at[c, :, pl.ds(pl.multiple_of(n * hn, hn), hn), :],
            send_sem=ns_sem.at[c, i], recv_sem=nr_sem.at[c, i],
            device_id=(w, there), device_id_type=MESH)

    def prepare(t):
        load_gate(t, 0).wait()
        high, low = split(real_form(g[t, 0]))
        left[t] = jnp.concatenate([high, low, high], axis=1)

    def rows(t, value):
        high, low = split(value.reshape(2 * order, order))
        stacked = jnp.concatenate([high, high, low], axis=0)
        return jnp.dot(left[t], stacked, preferred_element_type=F32)

    def columns(value):
        high, low = split(jnp.concatenate([value[:order], value[order:]], axis=1))
        stacked = jnp.concatenate([high, low, high], axis=1)
        return jnp.dot(stacked, right[...], preferred_element_type=F32)

    def first(c):
        load(c).wait()
        y[c] = rows(0, x[:, c]).reshape(2, order, order)

    def start_wide(c):
        for i in range(wide - 1):
            send_wide(c, i).start()

    prepare(0)
    first(0)
    pl.semaphore_wait(barrier, wide + narrow - 2)
    start_wide(0)

    @pl.loop(1, slabs)
    def _(c):
        first(c)
        start_wide(c)

    prepare(1)
    for t in range(3):
        load_gate(t, 1).wait()
    product = g[0, 1].reshape(2 * order, order)
    for t in (1, 2):
        product = jnp.dot(real_form(g[t, 1]), product, precision=precise, preferred_element_type=F32)
    re, im = product[:order].T, product[order:].T
    high, low = split(jnp.concatenate(
        [jnp.concatenate([re, im], axis=1), jnp.concatenate([-im, re], axis=1)], axis=0))
    right[...] = jnp.concatenate([high, high, low], axis=0)
    prepare(2)

    def second(c, with_columns):
        own = pl.ds(pl.multiple_of(w * hw, hw), hw)
        yr[c, :, own, :] = y[c, :, own, :]
        for i in range(wide - 1):
            send_wide(c, i).wait_recv()
        value = rows(1, yr[c])
        if with_columns:
            value = columns(value)
            z[c, 0] = value[:, :order]
            z[c, 1] = value[:, order:]
        else:
            z[c] = value.reshape(2, order, order)
        for i in range(narrow - 1):
            send_narrow(c, i).start()

    second(0, False)

    @pl.loop(1, slabs)
    def _(c):
        second(c, True)

    def third(c, with_columns):
        own = pl.ds(pl.multiple_of(n * hn, hn), hn)
        zr[c, :, own, :] = z[c, :, own, :]
        for i in range(narrow - 1):
            send_narrow(c, i).wait_recv()
        value = rows(2, zr[c])
        if with_columns:
            value = columns(value)
            out[0, c] = value[:, :order]
            out[1, c] = value[:, order:]
        else:
            out[0, c] = value[:order]
            out[1, c] = value[order:]

    third(0, True)

    @pl.loop(1, slabs)
    def _(c):
        third(c, False)

    @pl.loop(0, slabs)
    def _(c):
        for i in range(wide - 1):
            send_wide(c, i).wait_send()
        for i in range(narrow - 1):
            send_narrow(c, i).wait_send()


def fused(wide, narrow, amplitudes, gates):
    layout = amplitudes.shape
    slabs, order = layout[1], layout[4]
    vector = amplitudes.reshape(2, slabs, order, order)
    slab_buffer = pltpu.VMEM((slabs, 2, order, order), F32)
    result = pl.pallas_call(
        functools.partial(kernel, wide, narrow),
        out_shape=jax.ShapeDtypeStruct(vector.shape, F32),
        in_specs=[pl.BlockSpec(memory_space=pl.ANY)] * 2,
        out_specs=pl.BlockSpec(memory_space=pltpu.VMEM),
        scratch_shapes=[
            pltpu.VMEM(vector.shape, F32),
            pltpu.VMEM(gates.shape, F32),
            slab_buffer, slab_buffer, slab_buffer, slab_buffer,
            pltpu.VMEM((3, 2 * order, 6 * order), BF16),
            pltpu.VMEM((6 * order, 2 * order), BF16),
            pltpu.SemaphoreType.DMA((slabs,)),
            pltpu.SemaphoreType.DMA((3, 2)),
            pltpu.SemaphoreType.DMA((slabs, wide - 1)),
            pltpu.SemaphoreType.DMA((slabs, wide - 1)),
            pltpu.SemaphoreType.DMA((slabs, narrow - 1)),
            pltpu.SemaphoreType.DMA((slabs, narrow - 1)),
        ],
        compiler_params=pltpu.CompilerParams(
            collective_id=0, has_side_effects=True, vmem_limit_bytes=24 << 20),
    )(vector, gates)
    return result.reshape(layout)


def tiled(order, count):
    return count > 1 and count & (count - 1) == 0 and order % (8 * count) == 0


def solution(mesh):
    wide, narrow = mesh.shape["wide"], mesh.shape["narrow"]

    def shards(amplitudes, gates):
        order = amplitudes.shape[4]
        if tiled(order, wide) and tiled(order, narrow) and wide * narrow <= 128:
            return fused(wide, narrow, amplitudes, gates)
        return plain(amplitudes, gates)

    return jax.shard_map(
        shards,
        mesh=mesh,
        in_specs=(P(None, None, "wide", "narrow", None, None), P()),
        out_specs=P(None, None, "wide", "narrow", None, None),
        check_vma=False,
    )
```

time: 62.6 us -> 39.6 us (0.63)
  waiting for transfers between devices: 38.3 us -> 0 us
  Pallas kernels: 0 us -> 36.1 us
  starting transfers between devices: 10.1 us -> 0 us
  matrix products: 6.91 us -> 0 us
  local copies, waits for them, and re-layouts: 6.33 us -> 3.33 us
    all_to_all x2 -> x0, waiting for transfers between devices: 38.3 us -> none  [the longest x1 22.9 us: shards(): lax.all_to_all(resident, 'narrow', split_axis=4, concat_axis=3, tiled=True)]
    pallas_call x0 -> x1, Pallas kernels: none -> 36.1 us  [fused(): pl.pallas_call(functools.partial(kernel, wide, narrow), out_shape=jax.Sha...]
    all_to_all x2 -> x0, starting transfers between devices: 10.1 us -> none  [the longest x1 5.2 us: shards(): lax.all_to_all(resident, 'wide', split_axis=4, concat_axis=2, tiled=True)]
    dot_general x6 -> x0, matrix products: 6.91 us -> none  [the longest x3 3.84 us: on_rows(): jnp.einsum('cdjk,drkb->crjb', blocks(matrix), vector, precision=precise)]
    reshape x3 -> x0, local copies, waits for them, and re-layouts: 4.63 us -> none  [the longest x1 1.78 us: shards(): resident = vector.reshape(layout)]
    unnamed x4 -> x5, local copies, waits for them, and re-layouts: 0.37 us -> 3.33 us
    squeeze x1 -> x0, local copies, waits for them, and re-layouts: 1.34 us -> none  [blocks(): matrix[1]]
  transfers between devices with their start and end apart: 2 -> 0, of which waited for: 2 -> 0; matrix products, arithmetic and copies ran while one was open for 0% -> 0% of each run, Pallas kernels for 0% -> 0%
where the time goes in v1:
time: 39.6 us; the launch traced here: 39.4 us
  Pallas kernels  36.1 us (91%)
  local copies, waits for them, and re-layouts  3.33 us (8%)
    pallas_call x1, Pallas kernels, fused(): pl.pallas_call(functools.partial(kernel, wide, narrow), out_shape=jax.Sha...  36.1 us
    unnamed x5, local copies, waits for them, and re-layouts  3.33 us

profile of v1, /device:TPU:0, one launch (start us, length us, event | category | flops | bytes accessed | tf_op | source)
XLA Modules:
  0.0 39.4 jit_solution(7124418060333255836)
XLA Ops:
  0.0 0.0 copy-start
  0.0 1.2 %copy-done = f32[2,8,1,1,128,128]{5,4,3,2,1,0:T(8,128)S(1)} copy-done((f32[2,8,1,1,128,128]{5,4,3,2,1,0:T(8,128)S(1)}, f32[2,8,1,1,128,128]{5,4,3,2,1,0:T(8,128)}, u32[]{:S(2)}) %copy-start) | copy-done | bytes 1048600
  1.2 0.0 copy-start.1
  1.2 1.1 %copy-done.1 = f32[3,2,2,128,128]{4,3,2,1,0:T(8,128)S(1)} copy-done((f32[3,2,2,128,128]{4,3,2,1,0:T(8,128)S(1)}, f32[3,2,2,128,128]{4,3,2,1,0:T(8,128)}, u32[]{:S(2)}) %copy-start.1) | copy-done | bytes 786456
  2.4 36.1 %shard_map.28 = f32[2,8,128,128]{3,2,1,0:T(8,128)S(1)} custom-call(f32[2,8,128,128]{3,2,1,0:T(8,128)S(1)} %bitcast.5, f32[3,2,2,128,128]{4,3,2,1,0:T(8,128)S(1)} %copy-done.1), custom_call_target="tpu_custom_call" | custom-call | tf_op jit(solution)/shard_map/pallas_call | solution.py:213
  38.4 1.0 %copy.5 = f32[2,8,1,1,128,128]{5,4,3,2,1,0:T(8,128)} copy(f32[2,8,1,1,128,128]{5,4,3,2,1,0:T(8,128)S(1)} %bitcast.4) | data formatting | bytes 2097152
Async XLA Ops:
  0.0 1.2 %copy-start = (f32[2,8,1,1,128,128]{5,4,3,2,1,0:T(8,128)S(1)}, f32[2,8,1,1,128,128]{5,4,3,2,1,0:T(8,128)}, u32[]{:S(2)}) copy-start(f32[2,8,1,1,128,128]{5,4,3,2,1,0:T(8,128)} %param.2) | copy-start | bytes 3145732
  1.2 1.1 %copy-start.1 = (f32[3,2,2,128,128]{4,3,2,1,0:T(8,128)S(1)}, f32[3,2,2,128,128]{4,3,2,1,0:T(8,128)}, u32[]{:S(2)}) copy-start(f32[3,2,2,128,128]{4,3,2,1,0:T(8,128)} %gates.1) | copy-start | bytes 2359300

commit v2 on v1

--- a/solution.py
+++ b/solution.py
@@ -138,23 +138,12 @@
     first(0)
     pl.semaphore_wait(barrier, wide + narrow - 2)
     start_wide(0)
+    prepare(1)
 
     @pl.loop(1, slabs)
     def _(c):
         first(c)
         start_wide(c)
-
-    prepare(1)
-    for t in range(3):
-        load_gate(t, 1).wait()
-    product = g[0, 1].reshape(2 * order, order)
-    for t in (1, 2):
-        product = jnp.dot(real_form(g[t, 1]), product, precision=precise, preferred_element_type=F32)
-    re, im = product[:order].T, product[order:].T
-    high, low = split(jnp.concatenate(
-        [jnp.concatenate([re, im], axis=1), jnp.concatenate([-im, re], axis=1)], axis=0))
-    right[...] = jnp.concatenate([high, high, low], axis=0)
-    prepare(2)
 
     def second(c, with_columns):
         own = pl.ds(pl.multiple_of(w * hw, hw), hw)
@@ -172,6 +161,17 @@
             send_narrow(c, i).start()
 
     second(0, False)
+
+    for t in range(3):
+        load_gate(t, 1).wait()
+    product = g[0, 1].reshape(2 * order, order)
+    for t in (1, 2):
+        product = jnp.dot(real_form(g[t, 1]), product, precision=precise, preferred_element_type=F32)
+    re, im = product[:order].T, product[order:].T
+    high, low = split(jnp.concatenate(
+        [jnp.concatenate([re, im], axis=1), jnp.concatenate([-im, re], axis=1)], axis=0))
+    right[...] = jnp.concatenate([high, high, low], axis=0)
+    prepare(2)
 
     @pl.loop(1, slabs)
     def _(c):
@@ -230,7 +230,7 @@
         ],
         compiler_params=pltpu.CompilerParams(
             collective_id=0, has_side_effects=True, vmem_limit_bytes=24 << 20),
-    )(vector, gates)
+    )(*[pltpu.with_memory_space_constraint(value, pltpu.HBM) for value in (vector, gates)])
     return result.reshape(layout)
 
 

time: 39.6 us -> 37 us (0.934)
  local copies, waits for them, and re-layouts: 3.33 us -> 0.97 us
    unnamed x5 -> x1, local copies, waits for them, and re-layouts: 3.33 us -> 0.97 us
where the time goes in v2:
time: 37 us; the launch traced here: 36.9 us
  Pallas kernels  35.9 us (97%)
  local copies, waits for them, and re-layouts  0.97 us (3%)
    pallas_call x1, Pallas kernels, fused(): pl.pallas_call(functools.partial(kernel, wide, narrow), out_shape=jax.Sha...  35.9 us
    unnamed x1, local copies, waits for them, and re-layouts  0.97 us

profile of v2, /device:TPU:0, one launch (start us, length us, event | category | flops | bytes accessed | tf_op | source)
XLA Modules:
  0.0 36.9 jit_solution(1307820030653671182)
XLA Ops:
  0.0 35.9 %shard_map.28 = f32[2,8,128,128]{3,2,1,0:T(8,128)S(1)} custom-call(f32[2,8,128,128]{3,2,1,0:T(8,128)} %bitcast.5, f32[3,2,2,128,128]{4,3,2,1,0:T(8,128)} %gates.1), custom_call_target="tpu_custom_call" | custom-call | tf_op jit(solution)/shard_map/pallas_call | solution.py:213
  35.9 1.0 %copy.5 = f32[2,8,1,1,128,128]{5,4,3,2,1,0:T(8,128)} copy(f32[2,8,1,1,128,128]{5,4,3,2,1,0:T(8,128)S(1)} %bitcast.4) | data formatting | bytes 2097152

commit v3 on v2

--- a/solution.py
+++ b/solution.py
@@ -67,7 +67,7 @@
 
 
 def kernel(wide, narrow, amp, gates, out, x, g, y, yr, z, zr, left, right,
-           load_sem, gate_sem, ws_sem, wr_sem, ns_sem, nr_sem):
+           load_sem, gate_sem, ws_sem, wr_sem, ns_sem, nr_sem, ready_sem):
     slabs, order = x.shape[1], x.shape[2]
     hw, hn = order // wide, order // narrow
     w, n = lax.axis_index("wide"), lax.axis_index("narrow")
@@ -77,8 +77,17 @@
     barrier = pltpu.get_barrier_semaphore()
     for mask in wide_masks:
         pl.semaphore_signal(barrier, inc=1, device_id=(partner(w, mask, wide), n), device_id_type=MESH)
+    relay = narrow == 4
+    inner = n * (3 - n) // 2
     for mask in narrow_masks:
-        pl.semaphore_signal(barrier, inc=1, device_id=(w, partner(n, mask, narrow)), device_id_type=MESH)
+        def greet(mask=mask):
+            pl.semaphore_signal(
+                barrier, inc=1, device_id=(w, partner(n, mask, narrow)), device_id_type=MESH)
+        if relay and mask == 3:
+            pl.when(inner == 1)(greet)
+        else:
+            greet()
+    greetings = wide + narrow - 2 + (inner - 1 if relay else 0)
 
     def load(c):
         return pltpu.make_async_copy(amp.at[:, c], x.at[:, c], load_sem.at[c])
@@ -136,8 +145,11 @@
 
     prepare(0)
     first(0)
-    pl.semaphore_wait(barrier, wide + narrow - 2)
+    pl.semaphore_wait(barrier, greetings)
     start_wide(0)
+    if relay:
+        pl.semaphore_signal(
+            ready_sem, inc=1, device_id=(w, partner(n, 1, narrow)), device_id_type=MESH)
     prepare(1)
 
     @pl.loop(1, slabs)
@@ -160,6 +172,8 @@
         for i in range(narrow - 1):
             send_narrow(c, i).start()
 
+    if relay:
+        pl.semaphore_wait(ready_sem, 1)
     second(0, False)
 
     for t in range(3):
@@ -227,6 +241,7 @@
             pltpu.SemaphoreType.DMA((slabs, wide - 1)),
             pltpu.SemaphoreType.DMA((slabs, narrow - 1)),
             pltpu.SemaphoreType.DMA((slabs, narrow - 1)),
+            pltpu.SemaphoreType.REGULAR,
         ],
         compiler_params=pltpu.CompilerParams(
             collective_id=0, has_side_effects=True, vmem_limit_bytes=24 << 20),

time: 37 us -> 37 us (level)
  no operation moved by 1% of the time
where the time goes in v3:
time: 37 us; the launch traced here: 36.9 us
  Pallas kernels  35.9 us (97%)
  local copies, waits for them, and re-layouts  0.97 us (3%)
    pallas_call x1, Pallas kernels, fused(): pl.pallas_call(functools.partial(kernel, wide, narrow), out_shape=jax.Sha...  35.9 us
    unnamed x1, local copies, waits for them, and re-layouts  0.97 us

profile of v3, /device:TPU:0, one launch (start us, length us, event | category | flops | bytes accessed | tf_op | source)
XLA Modules:
  0.0 36.9 jit_solution(10025070154693985090)
XLA Ops:
  0.0 35.9 %shard_map.28 = f32[2,8,128,128]{3,2,1,0:T(8,128)S(1)} custom-call(f32[2,8,128,128]{3,2,1,0:T(8,128)} %bitcast.5, f32[3,2,2,128,128]{4,3,2,1,0:T(8,128)} %gates.1), custom_call_target="tpu_custom_call" | custom-call | tf_op jit(solution)/shard_map/pallas_call | solution.py:227
  35.9 1.0 %copy.5 = f32[2,8,1,1,128,128]{5,4,3,2,1,0:T(8,128)} copy(f32[2,8,1,1,128,128]{5,4,3,2,1,0:T(8,128)S(1)} %bitcast.4) | data formatting | bytes 2097152

commit v4 on v2

--- a/solution.py
+++ b/solution.py
@@ -11,6 +11,8 @@
 MESH = pl.DeviceIdType.MESH
 F32 = jnp.float32
 BF16 = jnp.bfloat16
+EARLY_AT = 4
+TAIL = 1
 
 
 def blocks(matrix):
@@ -66,9 +68,10 @@
     )
 
 
-def kernel(wide, narrow, amp, gates, out, x, g, y, yr, z, zr, left, right,
-           load_sem, gate_sem, ws_sem, wr_sem, ns_sem, nr_sem):
-    slabs, order = x.shape[1], x.shape[2]
+def kernel(wide, narrow, early, amp, gates, out, x, g, y, yr, z, zr, left, right,
+           load_sem, gate_sem, ws_sem, wr_sem, ns_sem, nr_sem, es_sem, er_sem):
+    slabs, order = amp.shape[1], amp.shape[2]
+    last = slabs - 1
     hw, hn = order // wide, order // narrow
     w, n = lax.axis_index("wide"), lax.axis_index("narrow")
     wide_masks = far_first(wide)
@@ -87,12 +90,14 @@
         return pltpu.make_async_copy(gates.at[t, k], g.at[t, k], gate_sem.at[t, k])
 
     load_gate(0, 0).start()
+    if early:
+        load(last).start()
     load(0).start()
     for t in range(3):
         for k in range(2):
             if (t, k) != (0, 0):
                 load_gate(t, k).start()
-    for c in range(1, slabs):
+    for c in range(1, last if early else slabs):
         load(c).start()
 
     def send_wide(c, i):
@@ -111,6 +116,21 @@
             send_sem=ns_sem.at[c, i], recv_sem=nr_sem.at[c, i],
             device_id=(w, there), device_id_type=MESH)
 
+    def send_early():
+        return pltpu.make_async_remote_copy(
+            src_ref=x.at[:, last], dst_ref=x.at[:, slabs],
+            send_sem=es_sem.at[0], recv_sem=er_sem.at[0],
+            device_id=(w, partner(n, 2, narrow)), device_id_type=MESH)
+
+    def send_half(k):
+        there = partner(n, 1, narrow)
+        index = partner(n, 2 * k, narrow)
+        return pltpu.make_async_remote_copy(
+            src_ref=z.at[last + k, :, pl.ds(pl.multiple_of(there * hn, hn), hn), :],
+            dst_ref=zr.at[last, :, pl.ds(pl.multiple_of(index * hn, hn), hn), :],
+            send_sem=es_sem.at[1 + k], recv_sem=er_sem.at[1 + k],
+            device_id=(w, there), device_id_type=MESH)
+
     def prepare(t):
         load_gate(t, 0).wait()
         high, low = split(real_form(g[t, 0]))
@@ -126,8 +146,9 @@
         stacked = jnp.concatenate([high, low, high], axis=1)
         return jnp.dot(stacked, right[...], preferred_element_type=F32)
 
-    def first(c):
-        load(c).wait()
+    def first(c, loaded=False):
+        if not loaded:
+            load(c).wait()
         y[c] = rows(0, x[:, c]).reshape(2, order, order)
 
     def start_wide(c):
@@ -136,16 +157,24 @@
 
     prepare(0)
     first(0)
+    if early:
+        load(last).wait()
     pl.semaphore_wait(barrier, wide + narrow - 2)
+    if early:
+        send_early().start()
     start_wide(0)
     prepare(1)
 
-    @pl.loop(1, slabs)
+    @pl.loop(1, last if early else slabs)
     def _(c):
         first(c)
         start_wide(c)
 
-    def second(c, with_columns):
+    if early:
+        first(last, True)
+        start_wide(last)
+
+    def second(c, with_columns, with_narrow=True):
         own = pl.ds(pl.multiple_of(w * hw, hw), hw)
         yr[c, :, own, :] = y[c, :, own, :]
         for i in range(wide - 1):
@@ -157,6 +186,8 @@
             z[c, 1] = value[:, order:]
         else:
             z[c] = value.reshape(2, order, order)
+        if not with_narrow:
+            return
         for i in range(narrow - 1):
             send_narrow(c, i).start()
 
@@ -173,15 +204,44 @@
     right[...] = jnp.concatenate([high, high, low], axis=0)
     prepare(2)
 
-    @pl.loop(1, slabs)
-    def _(c):
-        second(c, True)
-
-    def third(c, with_columns):
-        own = pl.ds(pl.multiple_of(n * hn, hn), hn)
-        zr[c, :, own, :] = z[c, :, own, :]
-        for i in range(narrow - 1):
-            send_narrow(c, i).wait_recv()
+    if early:
+        @pl.loop(1, EARLY_AT)
+        def _(c):
+            second(c, True)
+
+        send_early().wait_recv()
+        first(slabs, True)
+        start_wide(slabs)
+
+        @pl.loop(EARLY_AT, last - TAIL)
+        def _(c):
+            second(c, True)
+
+        @pl.loop(last, slabs + 1)
+        def _(c):
+            second(c, False, False)
+
+        for k in range(2):
+            send_half(k).start()
+            index = partner(n, 2 * k, narrow)
+            rows_to = pl.ds(pl.multiple_of(index * hn, hn), hn)
+            rows_from = pl.ds(pl.multiple_of(n * hn, hn), hn)
+            zr[last, :, rows_to, :] = z[last + k, :, rows_from, :]
+
+        @pl.loop(last - TAIL, last)
+        def _(c):
+            second(c, True)
+    else:
+        @pl.loop(1, slabs)
+        def _(c):
+            second(c, True)
+
+    def third(c, with_columns, exchanged=False):
+        if not exchanged:
+            own = pl.ds(pl.multiple_of(n * hn, hn), hn)
+            zr[c, :, own, :] = z[c, :, own, :]
+            for i in range(narrow - 1):
+                send_narrow(c, i).wait_recv()
         value = rows(2, zr[c])
         if with_columns:
             value = columns(value)
@@ -192,41 +252,65 @@
             out[1, c] = value[order:]
 
     third(0, True)
-
-    @pl.loop(1, slabs)
-    def _(c):
-        third(c, False)
-
-    @pl.loop(0, slabs)
+    if early:
+        @pl.loop(1, last - TAIL)
+        def _(c):
+            third(c, False)
+
+        for k in range(2):
+            send_half(k).wait_recv()
+        third(last, True, True)
+
+        @pl.loop(last - TAIL, last)
+        def _(c):
+            third(c, False)
+    else:
+        @pl.loop(1, slabs)
+        def _(c):
+            third(c, False)
+
+    @pl.loop(0, slabs + 1 if early else slabs)
     def _(c):
         for i in range(wide - 1):
             send_wide(c, i).wait_send()
+
+    @pl.loop(0, last if early else slabs)
+    def _(c):
         for i in range(narrow - 1):
             send_narrow(c, i).wait_send()
+
+    if early:
+        send_early().wait_send()
+        for k in range(2):
+            send_half(k).wait_send()
 
 
 def fused(wide, narrow, amplitudes, gates):
     layout = amplitudes.shape
     slabs, order = layout[1], layout[4]
     vector = amplitudes.reshape(2, slabs, order, order)
-    slab_buffer = pltpu.VMEM((slabs, 2, order, order), F32)
+    early = narrow == 4 and slabs > EARLY_AT + TAIL
+    slots = slabs + early
+    slab_buffer = pltpu.VMEM((slots, 2, order, order), F32)
     result = pl.pallas_call(
-        functools.partial(kernel, wide, narrow),
+        functools.partial(kernel, wide, narrow, early),
         out_shape=jax.ShapeDtypeStruct(vector.shape, F32),
         in_specs=[pl.BlockSpec(memory_space=pl.ANY)] * 2,
         out_specs=pl.BlockSpec(memory_space=pltpu.VMEM),
         scratch_shapes=[
-            pltpu.VMEM(vector.shape, F32),
+            pltpu.VMEM((2, slots, order, order), F32),
             pltpu.VMEM(gates.shape, F32),
             slab_buffer, slab_buffer, slab_buffer, slab_buffer,
             pltpu.VMEM((3, 2 * order, 6 * order), BF16),
             pltpu.VMEM((6 * order, 2 * order), BF16),
             pltpu.SemaphoreType.DMA((slabs,)),
             pltpu.SemaphoreType.DMA((3, 2)),
-            pltpu.SemaphoreType.DMA((slabs, wide - 1)),
-            pltpu.SemaphoreType.DMA((slabs, wide - 1)),
+            pltpu.SemaphoreType.DMA((slots, wide - 1)),
+            pltpu.SemaphoreType.DMA((slots, wide - 1)),
             pltpu.SemaphoreType.DMA((slabs, narrow - 1)),
             pltpu.SemaphoreType.DMA((slabs, narrow - 1)),
+            pltpu.SemaphoreType.DMA((3,)),
+            pltpu.SemaphoreType.DMA((3,)),
         ],
         compiler_params=pltpu.CompilerParams(
             collective_id=0, has_side_effects=True, vmem_limit_bytes=24 << 20),

time: 37 us -> 36.1 us (0.976)
  Pallas kernels: 35.9 us -> 35 us
    pallas_call x1, Pallas kernels: 35.9 us -> 35 us  [fused(): pl.pallas_call(functools.partial(kernel, wide, narrow, early), out_shape=...]
where the time goes in v4:
time: 36.1 us; the launch traced here: 36 us
  Pallas kernels  35 us (97%)
  local copies, waits for them, and re-layouts  0.97 us (3%)
    pallas_call x1, Pallas kernels, fused(): pl.pallas_call(functools.partial(kernel, wide, narrow, early), out_shape=...  35 us
    unnamed x1, local copies, waits for them, and re-layouts  0.97 us

profile of v4, /device:TPU:0, one launch (start us, length us, event | category | flops | bytes accessed | tf_op | source)
XLA Modules:
  0.0 36.0 jit_solution(15248988079360340073)
XLA Ops:
  0.0 35.0 %shard_map.28 = f32[2,8,128,128]{3,2,1,0:T(8,128)S(1)} custom-call(f32[2,8,128,128]{3,2,1,0:T(8,128)} %bitcast.5, f32[3,2,2,128,128]{4,3,2,1,0:T(8,128)} %gates.1), custom_call_target="tpu_custom_call" | custom-call | tf_op jit(solution)/shard_map/pallas_call | solution.py:295
  35.0 1.0 %copy.5 = f32[2,8,1,1,128,128]{5,4,3,2,1,0:T(8,128)} copy(f32[2,8,1,1,128,128]{5,4,3,2,1,0:T(8,128)S(1)} %bitcast.4) | data formatting | bytes 2097152

commit v5 on v4

--- a/solution.py
+++ b/solution.py
@@ -75,7 +75,7 @@
     hw, hn = order // wide, order // narrow
     w, n = lax.axis_index("wide"), lax.axis_index("narrow")
     wide_masks = far_first(wide)
-    narrow_masks = sorted(range(1, narrow), reverse=True)
+    narrow_masks = far_first(narrow)
 
     barrier = pltpu.get_barrier_semaphore()
     for mask in wide_masks:
@@ -120,11 +120,11 @@
         return pltpu.make_async_remote_copy(
             src_ref=x.at[:, last], dst_ref=x.at[:, slabs],
             send_sem=es_sem.at[0], recv_sem=er_sem.at[0],
-            device_id=(w, partner(n, 2, narrow)), device_id_type=MESH)
+            device_id=(w, partner(n, 3, narrow)), device_id_type=MESH)
 
     def send_half(k):
         there = partner(n, 1, narrow)
-        index = partner(n, 2 * k, narrow)
+        index = partner(n, 3 * k, narrow)
         return pltpu.make_async_remote_copy(
             src_ref=z.at[last + k, :, pl.ds(pl.multiple_of(there * hn, hn), hn), :],
             dst_ref=zr.at[last, :, pl.ds(pl.multiple_of(index * hn, hn), hn), :],
@@ -223,7 +223,7 @@
 
         for k in range(2):
             send_half(k).start()
-            index = partner(n, 2 * k, narrow)
+            index = partner(n, 3 * k, narrow)
             rows_to = pl.ds(pl.multiple_of(index * hn, hn), hn)
             rows_from = pl.ds(pl.multiple_of(n * hn, hn), hn)
             zr[last, :, rows_to, :] = z[last + k, :, rows_from, :]

time: 36.1 us -> 36.1 us (level)
  no operation moved by 1% of the time
where the time goes in v5:
time: 36.1 us; the launch traced here: 35.9 us
  Pallas kernels  35 us (97%)
  local copies, waits for them, and re-layouts  0.97 us (3%)
    pallas_call x1, Pallas kernels, fused(): pl.pallas_call(functools.partial(kernel, wide, narrow, early), out_shape=...  35 us
    unnamed x1, local copies, waits for them, and re-layouts  0.97 us

profile of v5, /device:TPU:0, one launch (start us, length us, event | category | flops | bytes accessed | tf_op | source)
XLA Modules:
  0.0 35.9 jit_solution(7975047246937648861)
XLA Ops:
  0.0 35.0 %shard_map.28 = f32[2,8,128,128]{3,2,1,0:T(8,128)S(1)} custom-call(f32[2,8,128,128]{3,2,1,0:T(8,128)} %bitcast.5, f32[3,2,2,128,128]{4,3,2,1,0:T(8,128)} %gates.1), custom_call_target="tpu_custom_call" | custom-call | tf_op jit(solution)/shard_map/pallas_call | solution.py:295
  35.0 1.0 %copy.5 = f32[2,8,1,1,128,128]{5,4,3,2,1,0:T(8,128)} copy(f32[2,8,1,1,128,128]{5,4,3,2,1,0:T(8,128)S(1)} %bitcast.4) | data formatting | bytes 2097152

commit v6 on v5

--- a/solution.py
+++ b/solution.py
@@ -75,7 +75,7 @@
     hw, hn = order // wide, order // narrow
     w, n = lax.axis_index("wide"), lax.axis_index("narrow")
     wide_masks = far_first(wide)
-    narrow_masks = far_first(narrow)
+    narrow_masks = list(range(1, narrow))
 
     barrier = pltpu.get_barrier_semaphore()
     for mask in wide_masks:

time: 36.1 us -> 35.7 us (0.989)
  Pallas kernels: 35 us -> 34.6 us
where the time goes in v6:
time: 35.7 us; the launch traced here: 35.6 us
  Pallas kernels  34.6 us (97%)
  local copies, waits for them, and re-layouts  0.97 us (3%)
    pallas_call x1, Pallas kernels, fused(): pl.pallas_call(functools.partial(kernel, wide, narrow, early), out_shape=...  34.6 us
    unnamed x1, local copies, waits for them, and re-layouts  0.97 us

profile of v6, /device:TPU:0, one launch (start us, length us, event | category | flops | bytes accessed | tf_op | source)
XLA Modules:
  0.0 35.6 jit_solution(15201525353279616078)
XLA Ops:
  0.0 34.6 %shard_map.28 = f32[2,8,128,128]{3,2,1,0:T(8,128)S(1)} custom-call(f32[2,8,128,128]{3,2,1,0:T(8,128)} %bitcast.5, f32[3,2,2,128,128]{4,3,2,1,0:T(8,128)} %gates.1), custom_call_target="tpu_custom_call" | custom-call | tf_op jit(solution)/shard_map/pallas_call | solution.py:295
  34.6 1.0 %copy.5 = f32[2,8,1,1,128,128]{5,4,3,2,1,0:T(8,128)} copy(f32[2,8,1,1,128,128]{5,4,3,2,1,0:T(8,128)S(1)} %bitcast.4) | data formatting | bytes 2097152
